TPU v7x, 512 devices: a whole 4x8x8 slice. The times are simulated.
512 devices in a mesh: wave: 4 (over y_hi, core), tx: 8 (over z), ty: 16 (over x, y_lo).
Axes of the slice: x: 4, y: 8 (y_hi: 2, y_lo: 4; y = y_hi * 4 + y_lo), z: 8, core: 2. Of those that a mesh axis runs over, the one named last changes fastest.
Arguments:
- initial_fields: float32 [4, 2, 12, 128, 8192], P('wave', None, None, 'tx', 'ty'), may hold values from -6 to 6
- source_profiles: float32 [4, 2, 3, 8192], P('wave'), may hold values from -6 to 6
- source_waveforms: float32 [4, 2, 5], P('wave'), may hold values from -3 to 3
- material_map: int32 [128, 8192], P('tx', 'ty'), may hold values from 0 to 2
- design_density: float32 [128, 8192], P('tx', 'ty'), may hold values from 0 to 1
- material_table: float32 [3, 4], replicated, may hold values from 0.02 to 12, as said below
- plane_indices: int32 [2], replicated, may hold values from 0 to 127
- design_box: int32 [6], replicated, may hold values from 0 to 128, as said below
Outputs:
- density_gradient: float32 [128, 8192], P('tx', 'ty')
- final_electric: float32 [4, 2, 3, 128, 8192], P('wave', None, None, 'tx', 'ty')
Inputs may be any that keep to these rules, and one draw needn't show every extreme that they name: `material_map`: material ids are below 3. `material_table`: column 0 lies in [1, 12], column 1 in [0.5, 3], column 2 in [0.3, 1.5], column 3 in [0.02, 0.5]. `plane_indices`: entry 0 is the source plane of the forward run, entry 1 the monitor plane where the adjoint run's source enters. `design_box`: x0 <= 16, y0 <= 16, x1 = 128, y1 = 128, z0 = 0, z1 = 64.
All inputs are finite; a program needn't handle non-finite values.
Results may differ from a plain program's by a relative error of at most 0.0001.
Values sent between devices are 32-bit elements; how exact they have to be, the bound alone decides.
A program may use at most 64 MiB of HBM per device.

v0:
```python
import jax
import jax.numpy as jnp
from jax import lax
from jax.sharding import PartitionSpec as P

NZ = 64
STEPS = 5
NMAT = 3
time_step = 0.5
contrast = 2.0


def shifted_2(value, axis, steps):
    count = lax.axis_size(axis)
    initial, last = (max(0, -steps), min(count, count - steps))
    return lax.ppermute(value, axis, [(source, source + steps) for source in range(initial, last)])


def ahead_rows(values, border):
    return jnp.concatenate([values[:, 1:], border], axis=1)


def behind_rows(values, border):
    return jnp.concatenate([border, values[:, :-1]], axis=1)


def ahead_lines(values, border):
    width = border.shape[2]
    return jnp.concatenate([values[:, :, width:], border], axis=2)


def behind_lines(values, border):
    width = border.shape[2]
    return jnp.concatenate([border, values[:, :, :-width]], axis=2)


def ahead_depth(values, depth_last):
    shifted = jnp.concatenate([values[:, :, 1:], jnp.zeros_like(values[:, :, :1])], axis=2)
    return jnp.where(depth_last, 0.0, shifted)


def behind_depth(values, depth_first):
    shifted = jnp.concatenate([jnp.zeros_like(values[:, :, :1]), values[:, :, :-1]], axis=2)
    return jnp.where(depth_first, 0.0, shifted)


def curl_electric(field, rows_ahead, lines_ahead, depth_last):
    part_one, part_two, part_three = (field[:, 0], field[:, 1], field[:, 2])
    curl_one = (
        ahead_lines(part_three, lines_ahead[:, 1])
        - part_three
        - (ahead_depth(part_two, depth_last) - part_two)
    )
    curl_two = (
        ahead_depth(part_one, depth_last)
        - part_one
        - (ahead_rows(part_three, rows_ahead[:, 1]) - part_three)
    )
    curl_three = (
        ahead_rows(part_two, rows_ahead[:, 0])
        - part_two
        - (ahead_lines(part_one, lines_ahead[:, 0]) - part_one)
    )
    return jnp.stack([curl_one, curl_two, curl_three], axis=1)


def curl_magnetic(field, rows_behind, lines_behind, depth_first):
    part_one, part_two, part_three = (field[:, 0], field[:, 1], field[:, 2])
    curl_one = (
        part_three
        - behind_lines(part_three, lines_behind[:, 1])
        - (part_two - behind_depth(part_two, depth_first))
    )
    curl_two = (
        part_one
        - behind_depth(part_one, depth_first)
        - (part_three - behind_rows(part_three, rows_behind[:, 1]))
    )
    curl_three = (
        part_two
        - behind_rows(part_two, rows_behind[:, 0])
        - (part_one - behind_lines(part_one, lines_behind[:, 0]))
    )
    return jnp.stack([curl_one, curl_two, curl_three], axis=1)


def electric_borders(field):
    rows_ahead = shifted_2(field[:, 1:, :1, :], "tx", -1)
    flat_part = field[:, 0::2, :, :NZ].reshape(field.shape[0], 2, field.shape[2] * NZ)
    lines_ahead = shifted_2(flat_part, "ty", -1)
    return (rows_ahead, lines_ahead.reshape(field.shape[0], 2, field.shape[2], NZ))


def magnetic_borders(field):
    rows_behind = shifted_2(field[:, 1:, -1:, :], "tx", 1)
    flat_part = field[:, 0::2, :, -NZ:].reshape(field.shape[0], 2, field.shape[2] * NZ)
    lines_behind = shifted_2(flat_part, "ty", 1)
    return (rows_behind, lines_behind.reshape(field.shape[0], 2, field.shape[2], NZ))


def design_mask(grid_rows, grid_flat, design_box):
    lines = grid_flat // NZ
    depth_ids = grid_flat % NZ
    in_rows = (grid_rows >= design_box[0]) & (grid_rows < design_box[1])
    in_lines = (
        (lines >= design_box[2])
        & (lines < design_box[3])
        & (depth_ids >= design_box[4])
        & (depth_ids < design_box[5])
    )
    return (in_rows[:, None] & in_lines[None, :]).astype(jnp.float32)


def coefficients(material_map, design_density, material_table, inside_design):
    damping = material_table[:, 3]
    denom = 1.0 + 0.25 * damping
    decay = (1.0 - 0.25 * damping) / denom
    drive = material_table[:, 2] * material_table[:, 2] * time_step / denom
    coupled = drive * material_table[:, 1]
    permittivity = jnp.zeros(material_map.shape, jnp.float32)
    decay_map = jnp.zeros(material_map.shape, jnp.float32)
    drive_map = jnp.zeros(material_map.shape, jnp.float32)
    coupled_map = jnp.zeros(material_map.shape, jnp.float32)
    for material_id in range(NMAT):
        chosen = (material_map == material_id).astype(jnp.float32)
        permittivity = permittivity + chosen * material_table[material_id, 0]
        decay_map = decay_map + chosen * decay[material_id]
        drive_map = drive_map + chosen * drive[material_id]
        coupled_map = coupled_map + chosen * coupled[material_id]
    permittivity = permittivity + inside_design * design_density * contrast
    return jnp.stack([time_step / permittivity, decay_map, drive_map, coupled_map])


def advance(
    electric,
    magnetic,
    polarization,
    current,
    coeffs,
    inside,
    depth_last,
    depth_first,
    source,
    get_electric,
    get_magnetic,
):
    rows_ahead, lines_ahead = get_electric(electric)
    magnetic = (
        magnetic - time_step * curl_electric(electric, rows_ahead, lines_ahead, depth_last)
    ) * inside
    current = coeffs[1] * current + coeffs[3] * electric - coeffs[2] * polarization
    polarization = polarization + time_step * current
    rows_behind, lines_behind = get_magnetic(magnetic)
    electric = electric + coeffs[0] * (
        curl_magnetic(magnetic, rows_behind, lines_behind, depth_first) - current - source
    )
    return (electric, magnetic, polarization, current)


def on_device(
    initial_fields,
    source_profiles,
    source_waveforms,
    material_map,
    design_density,
    material_table,
    plane_indices,
    design_box,
):
    rows_here, flat_here = material_map.shape
    tile_row = lax.axis_index("tx")
    tile_col = lax.axis_index("ty")
    grid_rows = tile_row * rows_here + jnp.arange(rows_here, dtype=jnp.int32)
    grid_flat = tile_col * flat_here + jnp.arange(flat_here, dtype=jnp.int32)
    inside_design = design_mask(grid_rows, grid_flat, design_box)
    coeffs = coefficients(material_map, design_density, material_table, inside_design)
    fields = initial_fields[0]
    profiles = source_profiles[0]
    waveforms = source_waveforms[0]
    inside = 1.0
    profiles_here = lax.dynamic_slice_in_dim(profiles, tile_col * flat_here, flat_here, axis=2)
    depth_ids = grid_flat % NZ
    depth_last = depth_ids == NZ - 1
    depth_first = depth_ids == 0
    plane_rows = (grid_rows[None, :] == plane_indices[:, None]).astype(jnp.float32)
    electric = fields[:, 0:3]
    magnetic = fields[:, 3:6]
    polarization = fields[:, 6:9]
    current = fields[:, 9:12]
    forward_history = [electric[0]]
    adjoint_history = [electric[1]]
    for step_index in range(STEPS):
        source = (
            waveforms[:, step_index][:, None, None, None]
            * profiles_here[:, :, None, :]
            * plane_rows[:, None, :, None]
        )
        electric, magnetic, polarization, current = advance(
            electric,
            magnetic,
            polarization,
            current,
            coeffs,
            inside,
            depth_last,
            depth_first,
            source,
            electric_borders,
            magnetic_borders,
        )
        forward_history.append(electric[0])
        adjoint_history.append(electric[1])
    partial_value = jnp.zeros((rows_here, flat_here), jnp.float32)
    for pair_index in range(1, STEPS + 1):
        partial_value = partial_value + jnp.sum(
            adjoint_history[STEPS + 1 - pair_index]
            * (forward_history[pair_index] - forward_history[pair_index - 1]),
            axis=0,
        )
    collected = lax.psum(partial_value, "wave")
    density_gradient = contrast * inside_design * collected
    return (density_gradient, electric[None])


def solution(mesh):
    placed = (
        P("wave", None, None, "tx", "ty"),
        P("wave", None, None, None),
        P("wave", None, None),
        P("tx", "ty"),
        P("tx", "ty"),
        P(),
        P(),
        P(),
    )
    return jax.shard_map(
        on_device,
        mesh=mesh,
        in_specs=placed,
        out_specs=(P("tx", "ty"), P("wave", None, None, "tx", "ty")),
        check_vma=False,
    )
```

profile of v0, /device:TPU:212, one launch (start us, length us, event | category | flops | bytes accessed | tf_op | source)
XLA Modules:
  0.0 151.3 jit_solution(15769013824842356531)
XLA Ops:
  0.6 1.2 copy.212
  2.0 2.4 %collective-permute-start = (f32[2,2,1024]{2,0,1:T(2,128)S(1)}, f32[2,2,1024]{2,0,1:T(2,128)S(1)}, u32[]{:S(2)}, u32[]{:S(2)}) collective-permute-start(f32[2,2,1024]{2,0,1:T(2,128)S(1)} %reshape.295), channel_id=1, source_target_pairs={{1,0},{2,1},{3,2},{4,3},{5,4},{6,5},{7,6},{8,7},{9,8},{10,9},{11,1... | collective-permute-start | bytes 49160 | tf_op jit(solution)/shard_map/ppermute | solution.py:16
  4.3 1.9 %collective-permute-start.1 = (f32[2,2,1,512]{3,2,0,1:T(1,128)S(1)}, f32[2,2,1,512]{3,2,0,1:T(1,128)S(1)}, u32[]{:S(2)}, u32[]{:S(2)}) collective-permute-start(f32[2,2,1,512]{3,2,0,1:T(1,128)S(1)} %slice.789), channel_id=1, source_target_pairs={{16,0},{32,16},{48,32},{64,48},{80,64},{96,80},{112,96},{17,1},{33... | collective-permute-start | bytes 24584 | tf_op jit(solution)/shard_map/ppermute | solution.py:16
  9.9 1.2 compare_and_fusion.1
  11.8 2.5 %compare_and_fusion = pred[512]{0:T(512)(128)(4,1)S(1)} fusion(s32[]{:T(128)} %bitcast.5, s32[]{:T(128)} %bitcast.4, s32[]{:T(128)} %bitcast.3, s32[]{:T(128)} %bitcast.2, s32[]{:T(128)S(6)} %mul.416), kind=kLoop, calls=%fused_computation.258 | loop fusion | flops 13824 | bytes 532 | tf_op jit(solution)/shard_map/and | solution.py:106
  14.9 1.9 %fusion.80 = (f32[16,512]{1,0:T(8,128)S(1)}, pred[16,512]{1,0:T(8,128)(4,1)S(1)}, pred[16,512]{1,0:T(8,128)(4,1)S(1)}, pred[16,512]{1,0:T(8,128)(4,1)S(1)}) fusion(f32[16,512]{1,0:T(8,128)S(1)} %copy-done.9, f32[]{:T(128)} %bitcast.9, f32[]{:T(128)} %bitcast.8, f32[]{:T(128)} %bitcast.7, pred[512]{0:T(512)(128)(4,1)S(1)} %compare_and_fusion, ...), kind=kLoop, calls=%fused_computation.208 | loop fusion | flops 106496 | bytes 123420 | tf_op jit(solution)/shard_map/div | solution.py:131
  16.9 0.8 bitcast_multiply_fusion
  17.7 5.7 %select_add_fusion.2 = (f32[16,512]{1,0:T(8,128)S(1)}, f32[16,512]{1,0:T(8,128)S(1)}, f32[16,512]{1,0:T(8,128)S(1)}) fusion(pred[16,512]{1,0:T(8,128)(4,1)S(1)} %get-tuple-element.20, pred[16,512]{1,0:T(8,128)(4,1)S(1)} %get-tuple-element.19, pred[16,512]{1,0:T(8,128)(4,1)S(1)} %get-tuple-element.18, f32[]{:T(128)} %bitcast.30, f32[]{:T(128)} %bitcast.29, ...), kind=kLoop, calls=%fused_computation.212 | loop fusion | flops 122880 | bytes 122916 | tf_op jit(solution)/shard_map/add | solution.py:127
  24.3 3.5 %collective-permute-start.2 = (f32[2,2,1024]{2,0,1:T(2,128)S(1)}, f32[2,2,1024]{2,0,1:T(2,128)S(1)}, u32[]{:S(2)}, u32[]{:S(2)}) collective-permute-start(f32[2,2,1024]{2,0,1:T(2,128)S(1)} %reshape.297), channel_id=1, source_target_pairs={{0,1},{1,2},{2,3},{3,4},{4,5},{5,6},{6,7},{7,8},{8,9},{9,10},{10,1... | collective-permute-start | bytes 49160 | tf_op jit(solution)/shard_map/ppermute | solution.py:16
  27.8 5.5 %collective-permute-start.3 = (f32[2,2,1,512]{3,2,0,1:T(1,128)S(1)}, f32[2,2,1,512]{3,2,0,1:T(1,128)S(1)}, u32[]{:S(2)}, u32[]{:S(2)}) collective-permute-start(f32[2,2,1,512]{3,2,0,1:T(1,128)S(1)} %slice.802), channel_id=1, source_target_pairs={{0,16},{16,32},{32,48},{48,64},{64,80},{80,96},{96,112},{1,17},{17... | collective-permute-start | bytes 24584 | tf_op jit(solution)/shard_map/ppermute | solution.py:16
  33.3 1.3 collective-permute-done.3
  35.2 1.9 %collective-permute-start.5 = (f32[2,2,1,512]{3,1,2,0:T(2,128)S(1)}, f32[2,2,1,512]{3,1,2,0:T(2,128)S(1)}, u32[]{:S(2)}, u32[]{:S(2)}) collective-permute-start(f32[2,2,1,512]{3,1,2,0:T(2,128)S(1)} %copy.139), channel_id=1, source_target_pairs={{16,0},{32,16},{48,32},{64,48},{80,64},{96,80},{112,96},{17,1},{33... | collective-permute-start | bytes 24584 | tf_op jit(solution)/shard_map/ppermute | solution.py:16
  37.5 2.4 %collective-permute-start.4 = (f32[2,2,1024]{2,0,1:T(2,128)S(1)}, f32[2,2,1024]{2,0,1:T(2,128)S(1)}, u32[]{:S(2)}, u32[]{:S(2)}) collective-permute-start(f32[2,2,1024]{2,0,1:T(2,128)S(1)} %copy.82), channel_id=1, source_target_pairs={{1,0},{2,1},{3,2},{4,3},{5,4},{6,5},{7,6},{8,7},{9,8},{10,9},{11,1... | collective-permute-start | bytes 49160 | tf_op jit(solution)/shard_map/ppermute | solution.py:16
  39.8 2.4 %collective-permute-done.5 = f32[2,2,1,512]{3,1,2,0:T(2,128)S(1)} collective-permute-done((f32[2,2,1,512]{3,1,2,0:T(2,128)S(1)}, f32[2,2,1,512]{3,1,2,0:T(2,128)S(1)}, u32[]{:S(2)}, u32[]{:S(2)}) %collective-permute-start.5) | collective-permute-done | bytes 8224 | tf_op jit(solution)/shard_map/ppermute | solution.py:16
  42.3 3.1 %collective-permute-done.4 = f32[2,2,1024]{2,0,1:T(2,128)S(1)} collective-permute-done((f32[2,2,1024]{2,0,1:T(2,128)S(1)}, f32[2,2,1024]{2,0,1:T(2,128)S(1)}, u32[]{:S(2)}, u32[]{:S(2)}) %collective-permute-start.4) | collective-permute-done | bytes 16416 | tf_op jit(solution)/shard_map/ppermute | solution.py:16
  46.0 6.7 %collective-permute-start.6 = (f32[2,2,1024]{2,0,1:T(2,128)S(1)}, f32[2,2,1024]{2,0,1:T(2,128)S(1)}, u32[]{:S(2)}, u32[]{:S(2)}) collective-permute-start(f32[2,2,1024]{2,0,1:T(2,128)S(1)} %reshape.301), channel_id=1, source_target_pairs={{0,1},{1,2},{2,3},{3,4},{4,5},{5,6},{6,7},{7,8},{8,9},{9,10},{10,1... | collective-permute-start | bytes 49160 | tf_op jit(solution)/shard_map/ppermute | solution.py:16
  52.7 5.4 %collective-permute-start.7 = (f32[2,2,1,512]{3,2,0,1:T(1,128)S(1)}, f32[2,2,1,512]{3,2,0,1:T(1,128)S(1)}, u32[]{:S(2)}, u32[]{:S(2)}) collective-permute-start(f32[2,2,1,512]{3,2,0,1:T(1,128)S(1)} %slice.832), channel_id=1, source_target_pairs={{0,16},{16,32},{32,48},{48,64},{64,80},{80,96},{96,112},{1,17},{17... | collective-permute-start | bytes 24584 | tf_op jit(solution)/shard_map/ppermute | solution.py:16
  58.1 1.3 collective-permute-done.7
  60.1 1.9 %collective-permute-start.9 = (f32[2,2,1,512]{3,2,0,1:T(1,128)S(1)}, f32[2,2,1,512]{3,2,0,1:T(1,128)S(1)}, u32[]{:S(2)}, u32[]{:S(2)}) collective-permute-start(f32[2,2,1,512]{3,2,0,1:T(1,128)S(1)} %slice.847), channel_id=1, source_target_pairs={{16,0},{32,16},{48,32},{64,48},{80,64},{96,80},{112,96},{17,1},{33... | collective-permute-start | bytes 24584 | tf_op jit(solution)/shard_map/ppermute | solution.py:16
  62.4 1.9 %collective-permute-start.8 = (f32[2,2,1024]{2,0,1:T(2,128)S(1)}, f32[2,2,1024]{2,0,1:T(2,128)S(1)}, u32[]{:S(2)}, u32[]{:S(2)}) collective-permute-start(f32[2,2,1024]{2,0,1:T(2,128)S(1)} %copy.95), channel_id=1, source_target_pairs={{1,0},{2,1},{3,2},{4,3},{5,4},{6,5},{7,6},{8,7},{9,8},{10,9},{11,1... | collective-permute-start | bytes 49160 | tf_op jit(solution)/shard_map/ppermute | solution.py:16
  64.3 2.8 %collective-permute-done.9 = f32[2,2,1,512]{3,2,0,1:T(1,128)S(1)} collective-permute-done((f32[2,2,1,512]{3,2,0,1:T(1,128)S(1)}, f32[2,2,1,512]{3,2,0,1:T(1,128)S(1)}, u32[]{:S(2)}, u32[]{:S(2)}) %collective-permute-start.9) | collective-permute-done | bytes 8224 | tf_op jit(solution)/shard_map/ppermute | solution.py:16
  67.1 0.9 collective-permute-done.8
  68.7 4.6 %collective-permute-start.10 = (f32[2,2,1024]{2,0,1:T(2,128)S(1)}, f32[2,2,1024]{2,0,1:T(2,128)S(1)}, u32[]{:S(2)}, u32[]{:S(2)}) collective-permute-start(f32[2,2,1024]{2,0,1:T(2,128)S(1)} %reshape.305), channel_id=1, source_target_pairs={{0,1},{1,2},{2,3},{3,4},{4,5},{5,6},{6,7},{7,8},{8,9},{9,10},{10,1... | collective-permute-start | bytes 49160 | tf_op jit(solution)/shard_map/ppermute | solution.py:16
  73.3 5.4 %collective-permute-start.11 = (f32[2,2,1,512]{3,2,0,1:T(1,128)S(1)}, f32[2,2,1,512]{3,2,0,1:T(1,128)S(1)}, u32[]{:S(2)}, u32[]{:S(2)}) collective-permute-start(f32[2,2,1,512]{3,2,0,1:T(1,128)S(1)} %slice.860), channel_id=1, source_target_pairs={{0,16},{16,32},{32,48},{48,64},{64,80},{80,96},{96,112},{1,17},{17... | collective-permute-start | bytes 24584 | tf_op jit(solution)/shard_map/ppermute | solution.py:16
  78.7 1.3 collective-permute-done.11
  80.6 1.9 %collective-permute-start.13 = (f32[2,2,1,512]{3,1,2,0:T(2,128)S(1)}, f32[2,2,1,512]{3,1,2,0:T(2,128)S(1)}, u32[]{:S(2)}, u32[]{:S(2)}) collective-permute-start(f32[2,2,1,512]{3,1,2,0:T(2,128)S(1)} %copy.143), channel_id=1, source_target_pairs={{16,0},{32,16},{48,32},{64,48},{80,64},{96,80},{112,96},{17,1},{33... | collective-permute-start | bytes 24584 | tf_op jit(solution)/shard_map/ppermute | solution.py:16
  83.0 1.9 %collective-permute-start.12 = (f32[2,2,1024]{2,0,1:T(2,128)S(1)}, f32[2,2,1024]{2,0,1:T(2,128)S(1)}, u32[]{:S(2)}, u32[]{:S(2)}) collective-permute-start(f32[2,2,1024]{2,0,1:T(2,128)S(1)} %copy.107), channel_id=1, source_target_pairs={{1,0},{2,1},{3,2},{4,3},{5,4},{6,5},{7,6},{8,7},{9,8},{10,9},{11,1... | collective-permute-start | bytes 49160 | tf_op jit(solution)/shard_map/ppermute | solution.py:16
  84.9 2.7 %collective-permute-done.13 = f32[2,2,1,512]{3,1,2,0:T(2,128)S(1)} collective-permute-done((f32[2,2,1,512]{3,1,2,0:T(2,128)S(1)}, f32[2,2,1,512]{3,1,2,0:T(2,128)S(1)}, u32[]{:S(2)}, u32[]{:S(2)}) %collective-permute-start.13) | collective-permute-done | bytes 8224 | tf_op jit(solution)/shard_map/ppermute | solution.py:16
  87.6 1.0 collective-permute-done.12
  89.8 4.6 %collective-permute-start.14 = (f32[2,2,1024]{2,0,1:T(2,128)S(1)}, f32[2,2,1024]{2,0,1:T(2,128)S(1)}, u32[]{:S(2)}, u32[]{:S(2)}) collective-permute-start(f32[2,2,1024]{2,0,1:T(2,128)S(1)} %reshape.309), channel_id=1, source_target_pairs={{0,1},{1,2},{2,3},{3,4},{4,5},{5,6},{6,7},{7,8},{8,9},{9,10},{10,1... | collective-permute-start | bytes 49160 | tf_op jit(solution)/shard_map/ppermute | solution.py:16
  94.5 5.4 %collective-permute-start.15 = (f32[2,2,1,512]{3,2,0,1:T(1,128)S(1)}, f32[2,2,1,512]{3,2,0,1:T(1,128)S(1)}, u32[]{:S(2)}, u32[]{:S(2)}) collective-permute-start(f32[2,2,1,512]{3,2,0,1:T(1,128)S(1)} %slice.888), channel_id=1, source_target_pairs={{0,16},{16,32},{32,48},{48,64},{64,80},{80,96},{96,112},{1,17},{17... | collective-permute-start | bytes 24584 | tf_op jit(solution)/shard_map/ppermute | solution.py:16
  99.9 1.3 collective-permute-done.15
  103.0 0.7 slice_bitcast_fusion.4
  103.7 1.9 %collective-permute-start.17 = (f32[2,2,1,512]{3,2,0,1:T(1,128)}, f32[2,2,1,512]{3,2,0,1:T(1,128)}, u32[]{:S(2)}, u32[]{:S(2)}) collective-permute-start(f32[2,2,1,512]{3,2,0,1:T(1,128)} %slice.903), channel_id=1, source_target_pairs={{16,0},{32,16},{48,32},{64,48},{80,64},{96,80},{112,96},{17,1},{33... | collective-permute-start | bytes 24584 | tf_op jit(solution)/shard_map/ppermute | solution.py:16
  106.8 0.7 slice.899
  107.5 0.7 slice.901
  108.2 0.8 reshape.311
  109.1 1.9 %collective-permute-start.16 = (f32[2,2,1024]{2,0,1:T(2,128)S(1)}, f32[2,2,1024]{2,0,1:T(2,128)S(1)}, u32[]{:S(2)}, u32[]{:S(2)}) collective-permute-start(f32[2,2,1024]{2,0,1:T(2,128)S(1)} %copy.120), channel_id=1, source_target_pairs={{1,0},{2,1},{3,2},{4,3},{5,4},{6,5},{7,6},{8,7},{9,8},{10,9},{11,1... | collective-permute-start | bytes 49160 | tf_op jit(solution)/shard_map/ppermute | solution.py:16
  111.0 1.3 slice_bitcast_fusion.63
  112.3 2.6 %collective-permute-done.16 = f32[2,2,1024]{2,0,1:T(2,128)S(1)} collective-permute-done((f32[2,2,1024]{2,0,1:T(2,128)S(1)}, f32[2,2,1024]{2,0,1:T(2,128)S(1)}, u32[]{:S(2)}, u32[]{:S(2)}) %collective-permute-start.16) | collective-permute-done | bytes 16416 | tf_op jit(solution)/shard_map/ppermute | solution.py:16
  115.0 0.7 copy-done.15
  115.7 1.0 slice_bitcast_fusion.6
  117.7 0.7 copy-done.2
  118.8 4.5 %collective-permute-start.18 = (f32[2,2,1024]{2,0,1:T(2,128)S(1)}, f32[2,2,1024]{2,0,1:T(2,128)S(1)}, u32[]{:S(2)}, u32[]{:S(2)}) collective-permute-start(f32[2,2,1024]{2,0,1:T(2,128)S(1)} %copy.127), channel_id=1, source_target_pairs={{0,1},{1,2},{2,3},{3,4},{4,5},{5,6},{6,7},{7,8},{8,9},{9,10},{10,1... | collective-permute-start | bytes 49160 | tf_op jit(solution)/shard_map/ppermute | solution.py:16
  123.3 5.4 %collective-permute-start.19 = (f32[2,2,1,512]{3,2,1,0:T(1,128)S(1)}, f32[2,2,1,512]{3,2,1,0:T(1,128)S(1)}, u32[]{:S(2)}, u32[]{:S(2)}) collective-permute-start(f32[2,2,1,512]{3,2,1,0:T(1,128)S(1)} %slice.916), channel_id=1, source_target_pairs={{0,16},{16,32},{32,48},{48,64},{64,80},{80,96},{96,112},{1,17},{17... | collective-permute-start | bytes 24584 | tf_op jit(solution)/shard_map/ppermute | solution.py:16
  128.7 1.3 collective-permute-done.19
  132.5 18.1 %psum.7 = f32[16,512]{1,0:T(8,128)S(1)} all-reduce(f32[16,512]{1,0:T(8,128)S(1)} %add_add_fusion), channel_id=1, replica_groups=mesh['wave'=4,'tx'=8,'ty'=16] {'wave'}, use_global_device_ids=true, to_apply=%region_5.6 | all-reduce | flops 8192 | bytes 65536 | tf_op jit(solution)/shard_map/psum | solution.py:220
  150.6 0.7 fusion.77
  (220 shorter events, 17.7 us)
Async XLA Ops:
  2.0 21.7 %collective-permute-start = (f32[2,2,1024]{2,0,1:T(2,128)S(1)}, f32[2,2,1024]{2,0,1:T(2,128)S(1)}, u32[]{:S(2)}, u32[]{:S(2)}) collective-permute-start(f32[2,2,1024]{2,0,1:T(2,128)S(1)} %reshape.295), channel_id=1, source_target_pairs={{1,0},{2,1},{3,2},{4,3},{5,4},{6,5},{7,6},{8,7},{9,8},{10,9},{11,1... | collective-permute-start | bytes 49160 | tf_op jit(solution)/shard_map/ppermute | solution.py:16
  4.3 2.0 %copy-start.11 = (f32[3,4]{1,0:T(4,128)S(1)}, f32[3,4]{1,0:T(4,128)}, u32[]{:S(2)}) copy-start(f32[3,4]{1,0:T(4,128)} %param.13) | copy-start | bytes 148
  4.3 19.2 %collective-permute-start.1 = (f32[2,2,1,512]{3,2,0,1:T(1,128)S(1)}, f32[2,2,1,512]{3,2,0,1:T(1,128)S(1)}, u32[]{:S(2)}, u32[]{:S(2)}) collective-permute-start(f32[2,2,1,512]{3,2,0,1:T(1,128)S(1)} %slice.789), channel_id=1, source_target_pairs={{16,0},{32,16},{48,32},{64,48},{80,64},{96,80},{112,96},{17,1},{33... | collective-permute-start | bytes 24584 | tf_op jit(solution)/shard_map/ppermute | solution.py:16
  6.9 0.7 copy-start.13
  8.9 79.9 %copy-start.16 = (pred[512]{0:T(512)(128)(4,1)}, pred[512]{0:T(512)(128)(4,1)S(1)}, u32[]{:S(2)}) copy-start(pred[512]{0:T(512)(128)(4,1)S(1)} %broadcast_compare_fusion.3) | copy-start | bytes 1540
  9.0 0.7 copy-start.12
  9.0 2.8 %copy-start.25 = (s32[2]{0:T(128)S(1)}, s32[2]{0:T(128)}, u32[]{:S(2)}) copy-start(s32[2]{0:T(128)} %param.14) | copy-start | bytes 28
  9.6 5.3 %copy-start.9 = (f32[16,512]{1,0:T(8,128)S(1)}, f32[16,512]{1,0:T(8,128)}, u32[]{:S(2)}) copy-start(f32[16,512]{1,0:T(8,128)} %param.12) | copy-start | bytes 98308
  9.6 5.3 %copy-start.10 = (s32[16,512]{1,0:T(8,128)S(1)}, s32[16,512]{1,0:T(8,128)}, u32[]{:S(2)}) copy-start(s32[16,512]{1,0:T(8,128)} %param.11) | copy-start | bytes 98308
  11.1 3.2 %copy-start.21 = (pred[16]{0:T(512)(128)(4,1)}, pred[16]{0:T(512)(128)(4,1)S(1)}, u32[]{:S(2)}) copy-start(pred[16]{0:T(512)(128)(4,1)S(1)} %compare_and_fusion.1) | copy-start | bytes 52
  11.8 90.4 %copy-start.7 = (f32[2,16]{1,0:T(2,128)}, f32[2,16]{1,0:T(2,128)S(1)}, u32[]{:S(2)}) copy-start(f32[2,16]{1,0:T(2,128)S(1)} %compare_convert_fusion) | copy-start | bytes 388
  14.3 0.6 copy-start.23
  23.4 56.8 %copy-start.18 = (pred[512]{0:T(512)(128)(4,1)}, pred[512]{0:T(512)(128)(4,1)S(1)}, u32[]{:S(2)}) copy-start(pred[512]{0:T(512)(128)(4,1)S(1)} %broadcast_compare_fusion.4) | copy-start | bytes 1540
  24.3 10.3 %collective-permute-start.2 = (f32[2,2,1024]{2,0,1:T(2,128)S(1)}, f32[2,2,1024]{2,0,1:T(2,128)S(1)}, u32[]{:S(2)}, u32[]{:S(2)}) collective-permute-start(f32[2,2,1024]{2,0,1:T(2,128)S(1)} %reshape.297), channel_id=1, source_target_pairs={{0,1},{1,2},{2,3},{3,4},{4,5},{5,6},{6,7},{7,8},{8,9},{9,10},{10,1... | collective-permute-start | bytes 49160 | tf_op jit(solution)/shard_map/ppermute | solution.py:16
  27.8 6.8 %collective-permute-start.3 = (f32[2,2,1,512]{3,2,0,1:T(1,128)S(1)}, f32[2,2,1,512]{3,2,0,1:T(1,128)S(1)}, u32[]{:S(2)}, u32[]{:S(2)}) collective-permute-start(f32[2,2,1,512]{3,2,0,1:T(1,128)S(1)} %slice.802), channel_id=1, source_target_pairs={{0,16},{16,32},{32,48},{48,64},{64,80},{80,96},{96,112},{1,17},{17... | collective-permute-start | bytes 24584 | tf_op jit(solution)/shard_map/ppermute | solution.py:16
  35.2 7.0 %collective-permute-start.5 = (f32[2,2,1,512]{3,1,2,0:T(2,128)S(1)}, f32[2,2,1,512]{3,1,2,0:T(2,128)S(1)}, u32[]{:S(2)}, u32[]{:S(2)}) collective-permute-start(f32[2,2,1,512]{3,1,2,0:T(2,128)S(1)} %copy.139), channel_id=1, source_target_pairs={{16,0},{32,16},{48,32},{64,48},{80,64},{96,80},{112,96},{17,1},{33... | collective-permute-start | bytes 24584 | tf_op jit(solution)/shard_map/ppermute | solution.py:16
  37.5 7.9 %collective-permute-start.4 = (f32[2,2,1024]{2,0,1:T(2,128)S(1)}, f32[2,2,1024]{2,0,1:T(2,128)S(1)}, u32[]{:S(2)}, u32[]{:S(2)}) collective-permute-start(f32[2,2,1024]{2,0,1:T(2,128)S(1)} %copy.82), channel_id=1, source_target_pairs={{1,0},{2,1},{3,2},{4,3},{5,4},{6,5},{7,6},{8,7},{9,8},{10,9},{11,1... | collective-permute-start | bytes 49160 | tf_op jit(solution)/shard_map/ppermute | solution.py:16
  46.0 13.5 %collective-permute-start.6 = (f32[2,2,1024]{2,0,1:T(2,128)S(1)}, f32[2,2,1024]{2,0,1:T(2,128)S(1)}, u32[]{:S(2)}, u32[]{:S(2)}) collective-permute-start(f32[2,2,1024]{2,0,1:T(2,128)S(1)} %reshape.301), channel_id=1, source_target_pairs={{0,1},{1,2},{2,3},{3,4},{4,5},{5,6},{6,7},{7,8},{8,9},{9,10},{10,1... | collective-permute-start | bytes 49160 | tf_op jit(solution)/shard_map/ppermute | solution.py:16
  52.7 6.8 %collective-permute-start.7 = (f32[2,2,1,512]{3,2,0,1:T(1,128)S(1)}, f32[2,2,1,512]{3,2,0,1:T(1,128)S(1)}, u32[]{:S(2)}, u32[]{:S(2)}) collective-permute-start(f32[2,2,1,512]{3,2,0,1:T(1,128)S(1)} %slice.832), channel_id=1, source_target_pairs={{0,16},{16,32},{32,48},{48,64},{64,80},{80,96},{96,112},{1,17},{17... | collective-permute-start | bytes 24584 | tf_op jit(solution)/shard_map/ppermute | solution.py:16
  60.1 7.0 %collective-permute-start.9 = (f32[2,2,1,512]{3,2,0,1:T(1,128)S(1)}, f32[2,2,1,512]{3,2,0,1:T(1,128)S(1)}, u32[]{:S(2)}, u32[]{:S(2)}) collective-permute-start(f32[2,2,1,512]{3,2,0,1:T(1,128)S(1)} %slice.847), channel_id=1, source_target_pairs={{16,0},{32,16},{48,32},{64,48},{80,64},{96,80},{112,96},{17,1},{33... | collective-permute-start | bytes 24584 | tf_op jit(solution)/shard_map/ppermute | solution.py:16
  62.4 5.6 %collective-permute-start.8 = (f32[2,2,1024]{2,0,1:T(2,128)S(1)}, f32[2,2,1024]{2,0,1:T(2,128)S(1)}, u32[]{:S(2)}, u32[]{:S(2)}) collective-permute-start(f32[2,2,1024]{2,0,1:T(2,128)S(1)} %copy.95), channel_id=1, source_target_pairs={{1,0},{2,1},{3,2},{4,3},{5,4},{6,5},{7,6},{8,7},{9,8},{10,9},{11,1... | collective-permute-start | bytes 49160 | tf_op jit(solution)/shard_map/ppermute | solution.py:16
  68.7 11.4 %collective-permute-start.10 = (f32[2,2,1024]{2,0,1:T(2,128)S(1)}, f32[2,2,1024]{2,0,1:T(2,128)S(1)}, u32[]{:S(2)}, u32[]{:S(2)}) collective-permute-start(f32[2,2,1024]{2,0,1:T(2,128)S(1)} %reshape.305), channel_id=1, source_target_pairs={{0,1},{1,2},{2,3},{3,4},{4,5},{5,6},{6,7},{7,8},{8,9},{9,10},{10,1... | collective-permute-start | bytes 49160 | tf_op jit(solution)/shard_map/ppermute | solution.py:16
  73.3 6.8 %collective-permute-start.11 = (f32[2,2,1,512]{3,2,0,1:T(1,128)S(1)}, f32[2,2,1,512]{3,2,0,1:T(1,128)S(1)}, u32[]{:S(2)}, u32[]{:S(2)}) collective-permute-start(f32[2,2,1,512]{3,2,0,1:T(1,128)S(1)} %slice.860), channel_id=1, source_target_pairs={{0,16},{16,32},{32,48},{48,64},{64,80},{80,96},{96,112},{1,17},{17... | collective-permute-start | bytes 24584 | tf_op jit(solution)/shard_map/ppermute | solution.py:16
  80.6 7.0 %collective-permute-start.13 = (f32[2,2,1,512]{3,1,2,0:T(2,128)S(1)}, f32[2,2,1,512]{3,1,2,0:T(2,128)S(1)}, u32[]{:S(2)}, u32[]{:S(2)}) collective-permute-start(f32[2,2,1,512]{3,1,2,0:T(2,128)S(1)} %copy.143), channel_id=1, source_target_pairs={{16,0},{32,16},{48,32},{64,48},{80,64},{96,80},{112,96},{17,1},{33... | collective-permute-start | bytes 24584 | tf_op jit(solution)/shard_map/ppermute | solution.py:16
  83.0 5.6 %collective-permute-start.12 = (f32[2,2,1024]{2,0,1:T(2,128)S(1)}, f32[2,2,1024]{2,0,1:T(2,128)S(1)}, u32[]{:S(2)}, u32[]{:S(2)}) collective-permute-start(f32[2,2,1024]{2,0,1:T(2,128)S(1)} %copy.107), channel_id=1, source_target_pairs={{1,0},{2,1},{3,2},{4,3},{5,4},{6,5},{7,6},{8,7},{9,8},{10,9},{11,1... | collective-permute-start | bytes 49160 | tf_op jit(solution)/shard_map/ppermute | solution.py:16
  88.9 0.6 copy-start.1
  88.9 0.6 copy-start.3
  89.8 11.4 %collective-permute-start.14 = (f32[2,2,1024]{2,0,1:T(2,128)S(1)}, f32[2,2,1024]{2,0,1:T(2,128)S(1)}, u32[]{:S(2)}, u32[]{:S(2)}) collective-permute-start(f32[2,2,1024]{2,0,1:T(2,128)S(1)} %reshape.309), channel_id=1, source_target_pairs={{0,1},{1,2},{2,3},{3,4},{4,5},{5,6},{6,7},{7,8},{8,9},{9,10},{10,1... | collective-permute-start | bytes 49160 | tf_op jit(solution)/shard_map/ppermute | solution.py:16
  94.5 6.8 %collective-permute-start.15 = (f32[2,2,1,512]{3,2,0,1:T(1,128)S(1)}, f32[2,2,1,512]{3,2,0,1:T(1,128)S(1)}, u32[]{:S(2)}, u32[]{:S(2)}) collective-permute-start(f32[2,2,1,512]{3,2,0,1:T(1,128)S(1)} %slice.888), channel_id=1, source_target_pairs={{0,16},{16,32},{32,48},{48,64},{64,80},{80,96},{96,112},{1,17},{17... | collective-permute-start | bytes 24584 | tf_op jit(solution)/shard_map/ppermute | solution.py:16
  101.4 0.6 copy-start.19
  103.7 7.4 %collective-permute-start.17 = (f32[2,2,1,512]{3,2,0,1:T(1,128)}, f32[2,2,1,512]{3,2,0,1:T(1,128)}, u32[]{:S(2)}, u32[]{:S(2)}) collective-permute-start(f32[2,2,1,512]{3,2,0,1:T(1,128)} %slice.903), channel_id=1, source_target_pairs={{16,0},{32,16},{48,32},{64,48},{80,64},{96,80},{112,96},{17,1},{33... | collective-permute-start | bytes 24584 | tf_op jit(solution)/shard_map/ppermute | solution.py:16
  109.1 5.8 %collective-permute-start.16 = (f32[2,2,1024]{2,0,1:T(2,128)S(1)}, f32[2,2,1024]{2,0,1:T(2,128)S(1)}, u32[]{:S(2)}, u32[]{:S(2)}) collective-permute-start(f32[2,2,1024]{2,0,1:T(2,128)S(1)} %copy.120), channel_id=1, source_target_pairs={{1,0},{2,1},{3,2},{4,3},{5,4},{6,5},{7,6},{8,7},{9,8},{10,9},{11,1... | collective-permute-start | bytes 49160 | tf_op jit(solution)/shard_map/ppermute | solution.py:16
  115.0 0.7 copy-start.15
  116.6 0.7 copy-start.14
  116.7 0.8 copy-start.5
  116.7 0.9 copy-start.6
  116.7 0.8 copy-start.17
  117.6 0.8 copy-start.2
  117.6 0.9 copy-start.4
  118.8 11.2 %collective-permute-start.18 = (f32[2,2,1024]{2,0,1:T(2,128)S(1)}, f32[2,2,1024]{2,0,1:T(2,128)S(1)}, u32[]{:S(2)}, u32[]{:S(2)}) collective-permute-start(f32[2,2,1024]{2,0,1:T(2,128)S(1)} %copy.127), channel_id=1, source_target_pairs={{0,1},{1,2},{2,3},{3,4},{4,5},{5,6},{6,7},{7,8},{8,9},{9,10},{10,1... | collective-permute-start | bytes 49160 | tf_op jit(solution)/shard_map/ppermute | solution.py:16
  123.3 6.8 %collective-permute-start.19 = (f32[2,2,1,512]{3,2,1,0:T(1,128)S(1)}, f32[2,2,1,512]{3,2,1,0:T(1,128)S(1)}, u32[]{:S(2)}, u32[]{:S(2)}) collective-permute-start(f32[2,2,1,512]{3,2,1,0:T(1,128)S(1)} %slice.916), channel_id=1, source_target_pairs={{0,16},{16,32},{32,48},{48,64},{64,80},{80,96},{96,112},{1,17},{17... | collective-permute-start | bytes 24584 | tf_op jit(solution)/shard_map/ppermute | solution.py:16
  130.2 0.6 copy-start.20
  131.0 0.7 copy-start.8
  131.8 0.7 copy-start
  132.5 18.1 %copy-start.22 = (pred[16]{0:T(512)(128)(4,1)S(1)}, pred[16]{0:T(512)(128)(4,1)}, u32[]{:S(2)}) copy-start(pred[16]{0:T(512)(128)(4,1)} %copy-done.21) | copy-start | bytes 52
  132.5 18.1 %copy-start.24 = (pred[512]{0:T(512)(128)(4,1)S(1)}, pred[512]{0:T(512)(128)(4,1)}, u32[]{:S(2)}) copy-start(pred[512]{0:T(512)(128)(4,1)} %copy-done.23) | copy-start | bytes 1540
where the time goes:
time: 153 us; the launch traced here: 151 us
  starting transfers between devices  71.1 us (46%)
  waiting for transfers between devices  22.2 us (15%)
  local copies, waits for them, and re-layouts  21.2 us (14%)
  blocking collectives  18.1 us (12%)
  other arithmetic  17.2 us (11%)
  between operations  1.69 us (1%)
    ppermute x20, starting transfers between devices, shifted_2(): lax.ppermute(value, axis, [(source, source + steps) for source in range(i...  71.1 us
    ppermute x20, waiting for transfers between devices, shifted_2(): lax.ppermute(value, axis, [(source, source + steps) for source in range(i...  22.2 us
    psum x1, blocking collectives, on_device(): collected = lax.psum(partial_value, 'wave')  18.1 us
    unnamed x55, local copies, waits for them, and re-layouts  8.55 us
    add x1, other arithmetic, coefficients(): decay_map = decay_map + chosen * decay[material_id]  5.68 us
  transfers between devices with their start and end apart: 20, of which 12 were waited for; matrix products, arithmetic and copies ran while one was open for 14% of the time, Pallas kernels for 0%

commit v1 on v0

--- a/solution.py
+++ b/solution.py
@@ -217,7 +217,7 @@
             * (forward_history[pair_index] - forward_history[pair_index - 1]),
             axis=0,
         )
-    collected = lax.psum(partial_value, "wave")
+    collected = jnp.sum(lax.all_gather(partial_value, "wave"), axis=0)
     density_gradient = contrast * inside_design * collected
     return (density_gradient, electric[None])
 

time: 153 us -> 145 us (0.948)
  blocking collectives: 18.1 us -> 9.32 us
    psum x1 -> x0, blocking collectives: 18.1 us -> none  [on_device(): collected = lax.psum(partial_value, 'wave')]
    all_gather x0 -> x1, blocking collectives: none -> 9.32 us  [on_device(): collected = jnp.sum(lax.all_gather(partial_value, 'wave'), axis=0)]
  transfers between devices with their start and end apart: 20 -> 20, of which waited for: 12 -> 12; matrix products, arithmetic and copies ran while one was open for 14% -> 15% of each run, Pallas kernels for 0% -> 0%
where the time goes in v1:
time: 145 us; the launch traced here: 143 us
  starting transfers between devices  71.1 us (49%)
  waiting for transfers between devices  22.1 us (15%)
  local copies, waits for them, and re-layouts  21.8 us (15%)
  other arithmetic  17.2 us (12%)
  blocking collectives  9.32 us (6%)
  between operations  1.66 us (1%)
    ppermute x20, starting transfers between devices, shifted_2(): lax.ppermute(value, axis, [(source, source + steps) for source in range(i...  71.1 us
    ppermute x20, waiting for transfers between devices, shifted_2(): lax.ppermute(value, axis, [(source, source + steps) for source in range(i...  22.1 us
    all_gather x1, blocking collectives, on_device(): collected = jnp.sum(lax.all_gather(partial_value, 'wave'), axis=0)  9.32 us
    unnamed x55, local copies, waits for them, and re-layouts  9.21 us
    add x1, other arithmetic, coefficients(): decay_map = decay_map + chosen * decay[material_id]  5.68 us
  transfers between devices with their start and end apart: 20, of which 12 were waited for; matrix products, arithmetic and copies ran while one was open for 15% of the time, Pallas kernels for 0%

profile of v1, /device:TPU:212, one launch (start us, length us, event | category | flops | bytes accessed | tf_op | source)
XLA Modules:
  0.0 143.2 jit_solution(14777789026957997822)
XLA Ops:
  0.6 1.2 copy.277
  2.0 2.4 %collective-permute-start = (f32[2,2,1024]{2,0,1:T(2,128)S(1)}, f32[2,2,1024]{2,0,1:T(2,128)S(1)}, u32[]{:S(2)}, u32[]{:S(2)}) collective-permute-start(f32[2,2,1024]{2,0,1:T(2,128)S(1)} %reshape.331), channel_id=1, source_target_pairs={{1,0},{2,1},{3,2},{4,3},{5,4},{6,5},{7,6},{8,7},{9,8},{10,9},{11,1... | collective-permute-start | bytes 49160 | tf_op jit(solution)/shard_map/ppermute | solution.py:16
  4.3 1.9 %collective-permute-start.1 = (f32[2,2,1,512]{3,2,0,1:T(1,128)S(1)}, f32[2,2,1,512]{3,2,0,1:T(1,128)S(1)}, u32[]{:S(2)}, u32[]{:S(2)}) collective-permute-start(f32[2,2,1,512]{3,2,0,1:T(1,128)S(1)} %slice.789), channel_id=1, source_target_pairs={{16,0},{32,16},{48,32},{64,48},{80,64},{96,80},{112,96},{17,1},{33... | collective-permute-start | bytes 24584 | tf_op jit(solution)/shard_map/ppermute | solution.py:16
  9.9 1.2 compare_and_fusion.1
  11.8 2.5 %compare_and_fusion = pred[512]{0:T(512)(128)(4,1)S(1)} fusion(s32[]{:T(128)} %bitcast.5, s32[]{:T(128)} %bitcast.4, s32[]{:T(128)} %bitcast.3, s32[]{:T(128)} %bitcast.2, s32[]{:T(128)S(6)} %mul.416), kind=kLoop, calls=%fused_computation.258 | loop fusion | flops 13824 | bytes 532 | tf_op jit(solution)/shard_map/and | solution.py:106
  14.9 1.9 %fusion.80 = (f32[16,512]{1,0:T(8,128)S(1)}, pred[16,512]{1,0:T(8,128)(4,1)S(1)}, pred[16,512]{1,0:T(8,128)(4,1)S(1)}, pred[16,512]{1,0:T(8,128)(4,1)S(1)}) fusion(f32[16,512]{1,0:T(8,128)S(1)} %copy-done.9, f32[]{:T(128)} %bitcast.9, f32[]{:T(128)} %bitcast.8, f32[]{:T(128)} %bitcast.7, pred[512]{0:T(512)(128)(4,1)S(1)} %compare_and_fusion, ...), kind=kLoop, calls=%fused_computation.208 | loop fusion | flops 106496 | bytes 123420 | tf_op jit(solution)/shard_map/div | solution.py:131
  16.9 0.8 bitcast_multiply_fusion
  17.7 5.7 %select_add_fusion.2 = (f32[16,512]{1,0:T(8,128)S(1)}, f32[16,512]{1,0:T(8,128)S(1)}, f32[16,512]{1,0:T(8,128)S(1)}) fusion(pred[16,512]{1,0:T(8,128)(4,1)S(1)} %get-tuple-element.20, pred[16,512]{1,0:T(8,128)(4,1)S(1)} %get-tuple-element.19, pred[16,512]{1,0:T(8,128)(4,1)S(1)} %get-tuple-element.18, f32[]{:T(128)} %bitcast.30, f32[]{:T(128)} %bitcast.29, ...), kind=kLoop, calls=%fused_computation.212 | loop fusion | flops 122880 | bytes 122916 | tf_op jit(solution)/shard_map/add | solution.py:127
  24.3 3.5 %collective-permute-start.2 = (f32[2,2,1024]{2,0,1:T(2,128)S(1)}, f32[2,2,1024]{2,0,1:T(2,128)S(1)}, u32[]{:S(2)}, u32[]{:S(2)}) collective-permute-start(f32[2,2,1024]{2,0,1:T(2,128)S(1)} %reshape.333), channel_id=1, source_target_pairs={{0,1},{1,2},{2,3},{3,4},{4,5},{5,6},{6,7},{7,8},{8,9},{9,10},{10,1... | collective-permute-start | bytes 49160 | tf_op jit(solution)/shard_map/ppermute | solution.py:16
  27.8 5.5 %collective-permute-start.3 = (f32[2,2,1,512]{3,2,0,1:T(1,128)S(1)}, f32[2,2,1,512]{3,2,0,1:T(1,128)S(1)}, u32[]{:S(2)}, u32[]{:S(2)}) collective-permute-start(f32[2,2,1,512]{3,2,0,1:T(1,128)S(1)} %slice.802), channel_id=1, source_target_pairs={{0,16},{16,32},{32,48},{48,64},{64,80},{80,96},{96,112},{1,17},{17... | collective-permute-start | bytes 24584 | tf_op jit(solution)/shard_map/ppermute | solution.py:16
  33.3 1.3 collective-permute-done.3
  35.2 1.9 %collective-permute-start.5 = (f32[2,2,1,512]{3,1,2,0:T(2,128)S(1)}, f32[2,2,1,512]{3,1,2,0:T(2,128)S(1)}, u32[]{:S(2)}, u32[]{:S(2)}) collective-permute-start(f32[2,2,1,512]{3,1,2,0:T(2,128)S(1)} %copy.204), channel_id=1, source_target_pairs={{16,0},{32,16},{48,32},{64,48},{80,64},{96,80},{112,96},{17,1},{33... | collective-permute-start | bytes 24584 | tf_op jit(solution)/shard_map/ppermute | solution.py:16
  37.5 2.4 %collective-permute-start.4 = (f32[2,2,1024]{2,0,1:T(2,128)S(1)}, f32[2,2,1024]{2,0,1:T(2,128)S(1)}, u32[]{:S(2)}, u32[]{:S(2)}) collective-permute-start(f32[2,2,1024]{2,0,1:T(2,128)S(1)} %copy.147), channel_id=1, source_target_pairs={{1,0},{2,1},{3,2},{4,3},{5,4},{6,5},{7,6},{8,7},{9,8},{10,9},{11,1... | collective-permute-start | bytes 49160 | tf_op jit(solution)/shard_map/ppermute | solution.py:16
  39.8 2.4 %collective-permute-done.5 = f32[2,2,1,512]{3,1,2,0:T(2,128)S(1)} collective-permute-done((f32[2,2,1,512]{3,1,2,0:T(2,128)S(1)}, f32[2,2,1,512]{3,1,2,0:T(2,128)S(1)}, u32[]{:S(2)}, u32[]{:S(2)}) %collective-permute-start.5) | collective-permute-done | bytes 8224 | tf_op jit(solution)/shard_map/ppermute | solution.py:16
  42.3 3.1 %collective-permute-done.4 = f32[2,2,1024]{2,0,1:T(2,128)S(1)} collective-permute-done((f32[2,2,1024]{2,0,1:T(2,128)S(1)}, f32[2,2,1024]{2,0,1:T(2,128)S(1)}, u32[]{:S(2)}, u32[]{:S(2)}) %collective-permute-start.4) | collective-permute-done | bytes 16416 | tf_op jit(solution)/shard_map/ppermute | solution.py:16
  46.0 6.7 %collective-permute-start.6 = (f32[2,2,1024]{2,0,1:T(2,128)S(1)}, f32[2,2,1024]{2,0,1:T(2,128)S(1)}, u32[]{:S(2)}, u32[]{:S(2)}) collective-permute-start(f32[2,2,1024]{2,0,1:T(2,128)S(1)} %reshape.337), channel_id=1, source_target_pairs={{0,1},{1,2},{2,3},{3,4},{4,5},{5,6},{6,7},{7,8},{8,9},{9,10},{10,1... | collective-permute-start | bytes 49160 | tf_op jit(solution)/shard_map/ppermute | solution.py:16
  52.7 5.4 %collective-permute-start.7 = (f32[2,2,1,512]{3,2,0,1:T(1,128)S(1)}, f32[2,2,1,512]{3,2,0,1:T(1,128)S(1)}, u32[]{:S(2)}, u32[]{:S(2)}) collective-permute-start(f32[2,2,1,512]{3,2,0,1:T(1,128)S(1)} %slice.832), channel_id=1, source_target_pairs={{0,16},{16,32},{32,48},{48,64},{64,80},{80,96},{96,112},{1,17},{17... | collective-permute-start | bytes 24584 | tf_op jit(solution)/shard_map/ppermute | solution.py:16
  58.1 1.3 collective-permute-done.7
  60.1 1.9 %collective-permute-start.9 = (f32[2,2,1,512]{3,2,0,1:T(1,128)S(1)}, f32[2,2,1,512]{3,2,0,1:T(1,128)S(1)}, u32[]{:S(2)}, u32[]{:S(2)}) collective-permute-start(f32[2,2,1,512]{3,2,0,1:T(1,128)S(1)} %slice.847), channel_id=1, source_target_pairs={{16,0},{32,16},{48,32},{64,48},{80,64},{96,80},{112,96},{17,1},{33... | collective-permute-start | bytes 24584 | tf_op jit(solution)/shard_map/ppermute | solution.py:16
  62.4 1.9 %collective-permute-start.8 = (f32[2,2,1024]{2,0,1:T(2,128)S(1)}, f32[2,2,1024]{2,0,1:T(2,128)S(1)}, u32[]{:S(2)}, u32[]{:S(2)}) collective-permute-start(f32[2,2,1024]{2,0,1:T(2,128)S(1)} %copy.160), channel_id=1, source_target_pairs={{1,0},{2,1},{3,2},{4,3},{5,4},{6,5},{7,6},{8,7},{9,8},{10,9},{11,1... | collective-permute-start | bytes 49160 | tf_op jit(solution)/shard_map/ppermute | solution.py:16
  64.3 2.8 %collective-permute-done.9 = f32[2,2,1,512]{3,2,0,1:T(1,128)S(1)} collective-permute-done((f32[2,2,1,512]{3,2,0,1:T(1,128)S(1)}, f32[2,2,1,512]{3,2,0,1:T(1,128)S(1)}, u32[]{:S(2)}, u32[]{:S(2)}) %collective-permute-start.9) | collective-permute-done | bytes 8224 | tf_op jit(solution)/shard_map/ppermute | solution.py:16
  67.1 0.9 collective-permute-done.8
  68.6 4.6 %collective-permute-start.10 = (f32[2,2,1024]{2,0,1:T(2,128)S(1)}, f32[2,2,1024]{2,0,1:T(2,128)S(1)}, u32[]{:S(2)}, u32[]{:S(2)}) collective-permute-start(f32[2,2,1024]{2,0,1:T(2,128)S(1)} %reshape.341), channel_id=1, source_target_pairs={{0,1},{1,2},{2,3},{3,4},{4,5},{5,6},{6,7},{7,8},{8,9},{9,10},{10,1... | collective-permute-start | bytes 49160 | tf_op jit(solution)/shard_map/ppermute | solution.py:16
  73.3 5.4 %collective-permute-start.11 = (f32[2,2,1,512]{3,2,0,1:T(1,128)S(1)}, f32[2,2,1,512]{3,2,0,1:T(1,128)S(1)}, u32[]{:S(2)}, u32[]{:S(2)}) collective-permute-start(f32[2,2,1,512]{3,2,0,1:T(1,128)S(1)} %slice.860), channel_id=1, source_target_pairs={{0,16},{16,32},{32,48},{48,64},{64,80},{80,96},{96,112},{1,17},{17... | collective-permute-start | bytes 24584 | tf_op jit(solution)/shard_map/ppermute | solution.py:16
  78.7 1.3 collective-permute-done.11
  80.6 1.9 %collective-permute-start.13 = (f32[2,2,1,512]{3,1,2,0:T(2,128)S(1)}, f32[2,2,1,512]{3,1,2,0:T(2,128)S(1)}, u32[]{:S(2)}, u32[]{:S(2)}) collective-permute-start(f32[2,2,1,512]{3,1,2,0:T(2,128)S(1)} %copy.208), channel_id=1, source_target_pairs={{16,0},{32,16},{48,32},{64,48},{80,64},{96,80},{112,96},{17,1},{33... | collective-permute-start | bytes 24584 | tf_op jit(solution)/shard_map/ppermute | solution.py:16
  83.0 1.9 %collective-permute-start.12 = (f32[2,2,1024]{2,0,1:T(2,128)S(1)}, f32[2,2,1024]{2,0,1:T(2,128)S(1)}, u32[]{:S(2)}, u32[]{:S(2)}) collective-permute-start(f32[2,2,1024]{2,0,1:T(2,128)S(1)} %copy.172), channel_id=1, source_target_pairs={{1,0},{2,1},{3,2},{4,3},{5,4},{6,5},{7,6},{8,7},{9,8},{10,9},{11,1... | collective-permute-start | bytes 49160 | tf_op jit(solution)/shard_map/ppermute | solution.py:16
  84.9 2.7 %collective-permute-done.13 = f32[2,2,1,512]{3,1,2,0:T(2,128)S(1)} collective-permute-done((f32[2,2,1,512]{3,1,2,0:T(2,128)S(1)}, f32[2,2,1,512]{3,1,2,0:T(2,128)S(1)}, u32[]{:S(2)}, u32[]{:S(2)}) %collective-permute-start.13) | collective-permute-done | bytes 8224 | tf_op jit(solution)/shard_map/ppermute | solution.py:16
  87.6 1.0 collective-permute-done.12
  89.8 4.6 %collective-permute-start.14 = (f32[2,2,1024]{2,0,1:T(2,128)S(1)}, f32[2,2,1024]{2,0,1:T(2,128)S(1)}, u32[]{:S(2)}, u32[]{:S(2)}) collective-permute-start(f32[2,2,1024]{2,0,1:T(2,128)S(1)} %reshape.345), channel_id=1, source_target_pairs={{0,1},{1,2},{2,3},{3,4},{4,5},{5,6},{6,7},{7,8},{8,9},{9,10},{10,1... | collective-permute-start | bytes 49160 | tf_op jit(solution)/shard_map/ppermute | solution.py:16
  94.5 5.4 %collective-permute-start.15 = (f32[2,2,1,512]{3,2,0,1:T(1,128)S(1)}, f32[2,2,1,512]{3,2,0,1:T(1,128)S(1)}, u32[]{:S(2)}, u32[]{:S(2)}) collective-permute-start(f32[2,2,1,512]{3,2,0,1:T(1,128)S(1)} %slice.888), channel_id=1, source_target_pairs={{0,16},{16,32},{32,48},{48,64},{64,80},{80,96},{96,112},{1,17},{17... | collective-permute-start | bytes 24584 | tf_op jit(solution)/shard_map/ppermute | solution.py:16
  99.9 1.3 collective-permute-done.15
  102.9 0.7 slice_bitcast_fusion.4
  103.7 1.9 %collective-permute-start.17 = (f32[2,2,1,512]{3,2,0,1:T(1,128)}, f32[2,2,1,512]{3,2,0,1:T(1,128)}, u32[]{:S(2)}, u32[]{:S(2)}) collective-permute-start(f32[2,2,1,512]{3,2,0,1:T(1,128)} %slice.903), channel_id=1, source_target_pairs={{16,0},{32,16},{48,32},{64,48},{80,64},{96,80},{112,96},{17,1},{33... | collective-permute-start | bytes 24584 | tf_op jit(solution)/shard_map/ppermute | solution.py:16
  106.8 0.7 slice.899
  107.5 0.7 slice.901
  108.2 0.8 reshape.347
  109.1 1.9 %collective-permute-start.16 = (f32[2,2,1024]{2,0,1:T(2,128)S(1)}, f32[2,2,1024]{2,0,1:T(2,128)S(1)}, u32[]{:S(2)}, u32[]{:S(2)}) collective-permute-start(f32[2,2,1024]{2,0,1:T(2,128)S(1)} %copy.185), channel_id=1, source_target_pairs={{1,0},{2,1},{3,2},{4,3},{5,4},{6,5},{7,6},{8,7},{9,8},{10,9},{11,1... | collective-permute-start | bytes 49160 | tf_op jit(solution)/shard_map/ppermute | solution.py:16
  111.0 1.3 slice_bitcast_fusion.63
  112.3 2.6 %collective-permute-done.16 = f32[2,2,1024]{2,0,1:T(2,128)S(1)} collective-permute-done((f32[2,2,1024]{2,0,1:T(2,128)S(1)}, f32[2,2,1024]{2,0,1:T(2,128)S(1)}, u32[]{:S(2)}, u32[]{:S(2)}) %collective-permute-start.16) | collective-permute-done | bytes 16416 | tf_op jit(solution)/shard_map/ppermute | solution.py:16
  115.0 0.7 copy-done.15
  115.6 1.0 slice_bitcast_fusion.6
  117.7 0.7 copy-done.2
  118.8 4.5 %collective-permute-start.18 = (f32[2,2,1024]{2,0,1:T(2,128)S(1)}, f32[2,2,1024]{2,0,1:T(2,128)S(1)}, u32[]{:S(2)}, u32[]{:S(2)}) collective-permute-start(f32[2,2,1024]{2,0,1:T(2,128)S(1)} %copy.192), channel_id=1, source_target_pairs={{0,1},{1,2},{2,3},{3,4},{4,5},{5,6},{6,7},{7,8},{8,9},{9,10},{10,1... | collective-permute-start | bytes 49160 | tf_op jit(solution)/shard_map/ppermute | solution.py:16
  123.2 5.4 %collective-permute-start.19 = (f32[2,2,1,512]{3,2,1,0:T(1,128)S(1)}, f32[2,2,1,512]{3,2,1,0:T(1,128)S(1)}, u32[]{:S(2)}, u32[]{:S(2)}) collective-permute-start(f32[2,2,1,512]{3,2,1,0:T(1,128)S(1)} %slice.916), channel_id=1, source_target_pairs={{0,16},{16,32},{32,48},{48,64},{64,80},{80,96},{96,112},{1,17},{17... | collective-permute-start | bytes 24584 | tf_op jit(solution)/shard_map/ppermute | solution.py:16
  128.7 1.3 collective-permute-done.19
  132.5 9.3 %all-gather = f32[64,512]{1,0:T(8,128)S(1)} all-gather(f32[16,512]{1,0:T(8,128)S(1)} %add_add_fusion), channel_id=2, replica_groups=mesh['wave'=4,'tx'=8,'ty'=16] {'wave'}, dimensions={0}, use_global_device_ids=true | all-gather | bytes 163840 | tf_op jit(solution)/shard_map/all_gather | solution.py:220
  142.5 0.7 fusion.77
  (221 shorter events, 18.3 us)
Async XLA Ops:
  2.0 21.7 %collective-permute-start = (f32[2,2,1024]{2,0,1:T(2,128)S(1)}, f32[2,2,1024]{2,0,1:T(2,128)S(1)}, u32[]{:S(2)}, u32[]{:S(2)}) collective-permute-start(f32[2,2,1024]{2,0,1:T(2,128)S(1)} %reshape.331), channel_id=1, source_target_pairs={{1,0},{2,1},{3,2},{4,3},{5,4},{6,5},{7,6},{8,7},{9,8},{10,9},{11,1... | collective-permute-start | bytes 49160 | tf_op jit(solution)/shard_map/ppermute | solution.py:16
  4.3 2.0 %copy-start.11 = (f32[3,4]{1,0:T(4,128)S(1)}, f32[3,4]{1,0:T(4,128)}, u32[]{:S(2)}) copy-start(f32[3,4]{1,0:T(4,128)} %param.13) | copy-start | bytes 148
  4.3 19.2 %collective-permute-start.1 = (f32[2,2,1,512]{3,2,0,1:T(1,128)S(1)}, f32[2,2,1,512]{3,2,0,1:T(1,128)S(1)}, u32[]{:S(2)}, u32[]{:S(2)}) collective-permute-start(f32[2,2,1,512]{3,2,0,1:T(1,128)S(1)} %slice.789), channel_id=1, source_target_pairs={{16,0},{32,16},{48,32},{64,48},{80,64},{96,80},{112,96},{17,1},{33... | collective-permute-start | bytes 24584 | tf_op jit(solution)/shard_map/ppermute | solution.py:16
  6.9 0.7 copy-start.13
  8.9 79.9 %copy-start.16 = (pred[512]{0:T(512)(128)(4,1)}, pred[512]{0:T(512)(128)(4,1)S(1)}, u32[]{:S(2)}) copy-start(pred[512]{0:T(512)(128)(4,1)S(1)} %broadcast_compare_fusion.3) | copy-start | bytes 1540
  9.0 0.7 copy-start.12
  9.0 2.8 %copy-start.25 = (s32[2]{0:T(128)S(1)}, s32[2]{0:T(128)}, u32[]{:S(2)}) copy-start(s32[2]{0:T(128)} %param.14) | copy-start | bytes 28
  9.6 5.3 %copy-start.9 = (f32[16,512]{1,0:T(8,128)S(1)}, f32[16,512]{1,0:T(8,128)}, u32[]{:S(2)}) copy-start(f32[16,512]{1,0:T(8,128)} %param.12) | copy-start | bytes 98308
  9.6 5.3 %copy-start.10 = (s32[16,512]{1,0:T(8,128)S(1)}, s32[16,512]{1,0:T(8,128)}, u32[]{:S(2)}) copy-start(s32[16,512]{1,0:T(8,128)} %param.11) | copy-start | bytes 98308
  11.1 3.2 %copy-start.21 = (pred[16]{0:T(512)(128)(4,1)}, pred[16]{0:T(512)(128)(4,1)S(1)}, u32[]{:S(2)}) copy-start(pred[16]{0:T(512)(128)(4,1)S(1)} %compare_and_fusion.1) | copy-start | bytes 52
  11.8 90.4 %copy-start.7 = (f32[2,16]{1,0:T(2,128)}, f32[2,16]{1,0:T(2,128)S(1)}, u32[]{:S(2)}) copy-start(f32[2,16]{1,0:T(2,128)S(1)} %compare_convert_fusion) | copy-start | bytes 388
  14.3 0.6 copy-start.23
  23.4 56.8 %copy-start.18 = (pred[512]{0:T(512)(128)(4,1)}, pred[512]{0:T(512)(128)(4,1)S(1)}, u32[]{:S(2)}) copy-start(pred[512]{0:T(512)(128)(4,1)S(1)} %broadcast_compare_fusion.4) | copy-start | bytes 1540
  24.3 10.3 %collective-permute-start.2 = (f32[2,2,1024]{2,0,1:T(2,128)S(1)}, f32[2,2,1024]{2,0,1:T(2,128)S(1)}, u32[]{:S(2)}, u32[]{:S(2)}) collective-permute-start(f32[2,2,1024]{2,0,1:T(2,128)S(1)} %reshape.333), channel_id=1, source_target_pairs={{0,1},{1,2},{2,3},{3,4},{4,5},{5,6},{6,7},{7,8},{8,9},{9,10},{10,1... | collective-permute-start | bytes 49160 | tf_op jit(solution)/shard_map/ppermute | solution.py:16
  27.8 6.8 %collective-permute-start.3 = (f32[2,2,1,512]{3,2,0,1:T(1,128)S(1)}, f32[2,2,1,512]{3,2,0,1:T(1,128)S(1)}, u32[]{:S(2)}, u32[]{:S(2)}) collective-permute-start(f32[2,2,1,512]{3,2,0,1:T(1,128)S(1)} %slice.802), channel_id=1, source_target_pairs={{0,16},{16,32},{32,48},{48,64},{64,80},{80,96},{96,112},{1,17},{17... | collective-permute-start | bytes 24584 | tf_op jit(solution)/shard_map/ppermute | solution.py:16
  35.2 7.0 %collective-permute-start.5 = (f32[2,2,1,512]{3,1,2,0:T(2,128)S(1)}, f32[2,2,1,512]{3,1,2,0:T(2,128)S(1)}, u32[]{:S(2)}, u32[]{:S(2)}) collective-permute-start(f32[2,2,1,512]{3,1,2,0:T(2,128)S(1)} %copy.204), channel_id=1, source_target_pairs={{16,0},{32,16},{48,32},{64,48},{80,64},{96,80},{112,96},{17,1},{33... | collective-permute-start | bytes 24584 | tf_op jit(solution)/shard_map/ppermute | solution.py:16
  37.5 7.9 %collective-permute-start.4 = (f32[2,2,1024]{2,0,1:T(2,128)S(1)}, f32[2,2,1024]{2,0,1:T(2,128)S(1)}, u32[]{:S(2)}, u32[]{:S(2)}) collective-permute-start(f32[2,2,1024]{2,0,1:T(2,128)S(1)} %copy.147), channel_id=1, source_target_pairs={{1,0},{2,1},{3,2},{4,3},{5,4},{6,5},{7,6},{8,7},{9,8},{10,9},{11,1... | collective-permute-start | bytes 49160 | tf_op jit(solution)/shard_map/ppermute | solution.py:16
  46.0 13.5 %collective-permute-start.6 = (f32[2,2,1024]{2,0,1:T(2,128)S(1)}, f32[2,2,1024]{2,0,1:T(2,128)S(1)}, u32[]{:S(2)}, u32[]{:S(2)}) collective-permute-start(f32[2,2,1024]{2,0,1:T(2,128)S(1)} %reshape.337), channel_id=1, source_target_pairs={{0,1},{1,2},{2,3},{3,4},{4,5},{5,6},{6,7},{7,8},{8,9},{9,10},{10,1... | collective-permute-start | bytes 49160 | tf_op jit(solution)/shard_map/ppermute | solution.py:16
  52.7 6.8 %collective-permute-start.7 = (f32[2,2,1,512]{3,2,0,1:T(1,128)S(1)}, f32[2,2,1,512]{3,2,0,1:T(1,128)S(1)}, u32[]{:S(2)}, u32[]{:S(2)}) collective-permute-start(f32[2,2,1,512]{3,2,0,1:T(1,128)S(1)} %slice.832), channel_id=1, source_target_pairs={{0,16},{16,32},{32,48},{48,64},{64,80},{80,96},{96,112},{1,17},{17... | collective-permute-start | bytes 24584 | tf_op jit(solution)/shard_map/ppermute | solution.py:16
  60.1 7.0 %collective-permute-start.9 = (f32[2,2,1,512]{3,2,0,1:T(1,128)S(1)}, f32[2,2,1,512]{3,2,0,1:T(1,128)S(1)}, u32[]{:S(2)}, u32[]{:S(2)}) collective-permute-start(f32[2,2,1,512]{3,2,0,1:T(1,128)S(1)} %slice.847), channel_id=1, source_target_pairs={{16,0},{32,16},{48,32},{64,48},{80,64},{96,80},{112,96},{17,1},{33... | collective-permute-start | bytes 24584 | tf_op jit(solution)/shard_map/ppermute | solution.py:16
  62.4 5.6 %collective-permute-start.8 = (f32[2,2,1024]{2,0,1:T(2,128)S(1)}, f32[2,2,1024]{2,0,1:T(2,128)S(1)}, u32[]{:S(2)}, u32[]{:S(2)}) collective-permute-start(f32[2,2,1024]{2,0,1:T(2,128)S(1)} %copy.160), channel_id=1, source_target_pairs={{1,0},{2,1},{3,2},{4,3},{5,4},{6,5},{7,6},{8,7},{9,8},{10,9},{11,1... | collective-permute-start | bytes 49160 | tf_op jit(solution)/shard_map/ppermute | solution.py:16
  68.6 11.4 %collective-permute-start.10 = (f32[2,2,1024]{2,0,1:T(2,128)S(1)}, f32[2,2,1024]{2,0,1:T(2,128)S(1)}, u32[]{:S(2)}, u32[]{:S(2)}) collective-permute-start(f32[2,2,1024]{2,0,1:T(2,128)S(1)} %reshape.341), channel_id=1, source_target_pairs={{0,1},{1,2},{2,3},{3,4},{4,5},{5,6},{6,7},{7,8},{8,9},{9,10},{10,1... | collective-permute-start | bytes 49160 | tf_op jit(solution)/shard_map/ppermute | solution.py:16
  73.3 6.8 %collective-permute-start.11 = (f32[2,2,1,512]{3,2,0,1:T(1,128)S(1)}, f32[2,2,1,512]{3,2,0,1:T(1,128)S(1)}, u32[]{:S(2)}, u32[]{:S(2)}) collective-permute-start(f32[2,2,1,512]{3,2,0,1:T(1,128)S(1)} %slice.860), channel_id=1, source_target_pairs={{0,16},{16,32},{32,48},{48,64},{64,80},{80,96},{96,112},{1,17},{17... | collective-permute-start | bytes 24584 | tf_op jit(solution)/shard_map/ppermute | solution.py:16
  80.6 7.0 %collective-permute-start.13 = (f32[2,2,1,512]{3,1,2,0:T(2,128)S(1)}, f32[2,2,1,512]{3,1,2,0:T(2,128)S(1)}, u32[]{:S(2)}, u32[]{:S(2)}) collective-permute-start(f32[2,2,1,512]{3,1,2,0:T(2,128)S(1)} %copy.208), channel_id=1, source_target_pairs={{16,0},{32,16},{48,32},{64,48},{80,64},{96,80},{112,96},{17,1},{33... | collective-permute-start | bytes 24584 | tf_op jit(solution)/shard_map/ppermute | solution.py:16
  83.0 5.6 %collective-permute-start.12 = (f32[2,2,1024]{2,0,1:T(2,128)S(1)}, f32[2,2,1024]{2,0,1:T(2,128)S(1)}, u32[]{:S(2)}, u32[]{:S(2)}) collective-permute-start(f32[2,2,1024]{2,0,1:T(2,128)S(1)} %copy.172), channel_id=1, source_target_pairs={{1,0},{2,1},{3,2},{4,3},{5,4},{6,5},{7,6},{8,7},{9,8},{10,9},{11,1... | collective-permute-start | bytes 49160 | tf_op jit(solution)/shard_map/ppermute | solution.py:16
  88.9 0.6 copy-start.1
  88.9 0.6 copy-start.3
  89.8 11.4 %collective-permute-start.14 = (f32[2,2,1024]{2,0,1:T(2,128)S(1)}, f32[2,2,1024]{2,0,1:T(2,128)S(1)}, u32[]{:S(2)}, u32[]{:S(2)}) collective-permute-start(f32[2,2,1024]{2,0,1:T(2,128)S(1)} %reshape.345), channel_id=1, source_target_pairs={{0,1},{1,2},{2,3},{3,4},{4,5},{5,6},{6,7},{7,8},{8,9},{9,10},{10,1... | collective-permute-start | bytes 49160 | tf_op jit(solution)/shard_map/ppermute | solution.py:16
  94.5 6.8 %collective-permute-start.15 = (f32[2,2,1,512]{3,2,0,1:T(1,128)S(1)}, f32[2,2,1,512]{3,2,0,1:T(1,128)S(1)}, u32[]{:S(2)}, u32[]{:S(2)}) collective-permute-start(f32[2,2,1,512]{3,2,0,1:T(1,128)S(1)} %slice.888), channel_id=1, source_target_pairs={{0,16},{16,32},{32,48},{48,64},{64,80},{80,96},{96,112},{1,17},{17... | collective-permute-start | bytes 24584 | tf_op jit(solution)/shard_map/ppermute | solution.py:16
  101.4 0.6 copy-start.19
  103.7 7.4 %collective-permute-start.17 = (f32[2,2,1,512]{3,2,0,1:T(1,128)}, f32[2,2,1,512]{3,2,0,1:T(1,128)}, u32[]{:S(2)}, u32[]{:S(2)}) collective-permute-start(f32[2,2,1,512]{3,2,0,1:T(1,128)} %slice.903), channel_id=1, source_target_pairs={{16,0},{32,16},{48,32},{64,48},{80,64},{96,80},{112,96},{17,1},{33... | collective-permute-start | bytes 24584 | tf_op jit(solution)/shard_map/ppermute | solution.py:16
  109.1 5.8 %collective-permute-start.16 = (f32[2,2,1024]{2,0,1:T(2,128)S(1)}, f32[2,2,1024]{2,0,1:T(2,128)S(1)}, u32[]{:S(2)}, u32[]{:S(2)}) collective-permute-start(f32[2,2,1024]{2,0,1:T(2,128)S(1)} %copy.185), channel_id=1, source_target_pairs={{1,0},{2,1},{3,2},{4,3},{5,4},{6,5},{7,6},{8,7},{9,8},{10,9},{11,1... | collective-permute-start | bytes 49160 | tf_op jit(solution)/shard_map/ppermute | solution.py:16
  115.0 0.7 copy-start.15
  116.6 0.7 copy-start.14
  116.7 0.8 copy-start.5
  116.7 0.9 copy-start.6
  116.7 0.8 copy-start.17
  117.6 0.8 copy-start.2
  117.6 0.9 copy-start.4
  118.8 11.2 %collective-permute-start.18 = (f32[2,2,1024]{2,0,1:T(2,128)S(1)}, f32[2,2,1024]{2,0,1:T(2,128)S(1)}, u32[]{:S(2)}, u32[]{:S(2)}) collective-permute-start(f32[2,2,1024]{2,0,1:T(2,128)S(1)} %copy.192), channel_id=1, source_target_pairs={{0,1},{1,2},{2,3},{3,4},{4,5},{5,6},{6,7},{7,8},{8,9},{9,10},{10,1... | collective-permute-start | bytes 49160 | tf_op jit(solution)/shard_map/ppermute | solution.py:16
  123.2 6.8 %collective-permute-start.19 = (f32[2,2,1,512]{3,2,1,0:T(1,128)S(1)}, f32[2,2,1,512]{3,2,1,0:T(1,128)S(1)}, u32[]{:S(2)}, u32[]{:S(2)}) collective-permute-start(f32[2,2,1,512]{3,2,1,0:T(1,128)S(1)} %slice.916), channel_id=1, source_target_pairs={{0,16},{16,32},{32,48},{48,64},{64,80},{80,96},{96,112},{1,17},{17... | collective-permute-start | bytes 24584 | tf_op jit(solution)/shard_map/ppermute | solution.py:16
  130.2 0.6 copy-start.20
  130.9 0.7 copy-start.8
  131.8 0.7 copy-start
  141.8 0.7 copy-start.22
  141.8 0.7 copy-start.24
